TPU v7x, 256 devices: a whole 4x4x8 slice. The times are simulated.
256 devices in a mesh: gx: 64 (over x, z_hi, y, core), gy: 4 (over z_lo).
Axes of the slice: x: 4, y: 4, z: 8 (z_hi: 2, z_lo: 4; z = z_hi * 4 + z_lo), core: 2. Of those that a mesh axis runs over, the one named last changes fastest.
Arguments:
- velocity: float32 [3, 512, 64, 512], P(None, 'gx', None, 'gy'), may hold values from -6 to 6
- cotangent: float32 [3, 512, 64, 512], P(None, 'gx', None, 'gy'), may hold values from -6 to 6
- coefficient: float32 [512, 64, 512], P('gx', None, 'gy'), may hold values from 0.5 to 1.5
- level_profile: float32 [64], replicated, may hold values from 0.1 to 1
- vert_deriv: float32 [64, 64], replicated, may hold values from -0.75 to 0.75
- eigen_vectors: float32 [64, 64], replicated, may hold values from -0.75 to 0.75
- eigen_inverse: float32 [64, 64], replicated, may hold values from -0.75 to 0.75
- eigen_rates: float32 [64], replicated, may hold values from 0.25 to 4
Outputs:
- new_velocity: float32 [3, 512, 64, 512], P(None, 'gx', None, 'gy')
- adjoint_velocity: float32 [3, 512, 64, 512], P(None, 'gx', None, 'gy')
- viscosity_gradient: float32 [512, 64, 512], P('gx', None, 'gy')
All inputs are finite; a program needn't handle non-finite values.
Results may differ from a plain program's by a relative error of at most 0.00005.
Values sent between devices are 32-bit elements; how exact they have to be, the bound alone decides.
A program may use at most 128 MiB of HBM per device.

v0:
```python
import functools
import math

import jax
import jax.numpy as jnp
import ml_dtypes
import numpy as np
from jax import lax
from jax.experimental import pallas as pl
from jax.experimental.pallas import tpu as pltpu
from jax.sharding import PartitionSpec as P

MESH = pl.DeviceIdType.MESH
step_weight = 0.3 * 8.0 / 15.0
N = 512
HALF = N // 2
UNIT = 2.0 * math.pi / N
f32 = jnp.float32
bf16 = jnp.bfloat16


def basis():
    k = np.arange(HALF)[:, None]
    x = np.arange(N)[None, :]
    angle = (k * x % N) * (2.0 * np.pi / N)
    cos, sin = np.cos(angle), np.sin(angle)
    sin[0] = np.cos(np.pi * x[0])
    scale = np.full((HALF, 1), math.sqrt(2.0 / N))
    scale[0] = math.sqrt(1.0 / N)
    table = np.concatenate([scale * cos, scale * sin], axis=0)
    out = []
    for t in (table, table.T):
        high = t.astype(ml_dtypes.bfloat16)
        low = (t - high.astype(np.float64)).astype(ml_dtypes.bfloat16)
        out += [np.ascontiguousarray(high), np.ascontiguousarray(low)]
    return out


def split(v):
    high = v.astype(bf16)
    return high, (v - high.astype(f32)).astype(bf16)


def dot(a, b):
    return jnp.dot(a, b, preferred_element_type=f32)


def dot3(a_high, a_low, b_high, b_low):
    return dot(a_high, b_high) + (dot(a_high, b_low) + dot(a_low, b_high))


def lanes(shape):
    return lax.broadcasted_iota(jnp.int32, shape, len(shape) - 1)


def quad(m):
    high, low = split(m)
    odd = (lanes(m.shape) // 64) % 2 == 1
    return jnp.where(odd, low.astype(f32), high.astype(f32)).astype(bf16)


def apply(m4, f):
    high, low = split(f)
    return dot(m4, jnp.concatenate([high, high, low, low], axis=0))


def body_kernel(
    vel, cot, coef, prof, mats, rates, t_high, t_low, tt_high, tt_low,
    o_new, o_adj, o_grad,
    velp, cotv, coefv, lap, sec, grad, ycol, yhalo,
    send_z, recv_x, back_x, back_z, grp, grp_in, bck, bck_in,
    tab, ttab, m4,
    load_sem, out_sem, hx_send, hx_recv, hy_send, hy_recv,
    big_send, big_recv, grp_send, grp_recv, bck_send, bck_recv, ret_send, ret_recv,
):
    gx = lax.axis_index("gx")
    q = lax.axis_index("gy")
    core = gx % 2
    cy = (gx // 2) % 4
    cx = gx // 16
    cz = ((gx // 8) % 2) * 4 + q
    part = (cy % 2) * 2 + core
    level = (cx * 2 + cy // 2) * 8 + cz

    def gx_of(x, z, y, c):
        return ((x * 2 + z // 4) * 4 + y) * 2 + c

    def member(j):
        return (gx_of(cx, cz, (cy // 2) * 2 + j // 2, j % 2), q)

    east, west = ((gx + 1) % 64, q), ((gx + 63) % 64, q)
    north, south = (gx, (q + 1) % 4), (gx, (q + 3) % 4)

    barrier = pltpu.get_barrier_semaphore()

    def tell(dev):
        pl.semaphore_signal(barrier, inc=1, device_id=dev, device_id_type=MESH)

    def tell_source(t, carry):
        i = (gx + t) % 64

        @pl.when(jnp.logical_or(i != gx, q != part))
        def _():
            tell((i, part))

        return carry

    lax.fori_loop(0, 64, tell_source, 0)
    for d in range(1, 4):
        tell(member((part + d) % 4))
    for dev in (east, west, north, south):
        tell(dev)

    loads = [
        pltpu.make_async_copy(cot, cotv, load_sem.at[0]),
        pltpu.make_async_copy(vel, velp.at[:, pl.ds(1, 8)], load_sem.at[1]),
        pltpu.make_async_copy(coef, coefv, load_sem.at[2]),
        pltpu.make_async_copy(t_high, tab.at[0], load_sem.at[3]),
        pltpu.make_async_copy(t_low, tab.at[1], load_sem.at[4]),
        pltpu.make_async_copy(tt_high, ttab.at[0], load_sem.at[5]),
        pltpu.make_async_copy(tt_low, ttab.at[1], load_sem.at[6]),
    ]
    for copy in loads:
        copy.start()

    D, V, E, Dt, Vt, Et = (mats[i] for i in range(6))
    qD, qV, qE, qDt, qVt, qEt = (quad(m) for m in (D, V, E, Dt, Vt, Et))
    m4[0] = quad(-Vt)
    m4[1] = quad(apply(qVt, Dt))
    m4[2] = qD
    m4[3] = qE
    m4[4] = quad(apply(qE, D))
    m4[5] = qEt
    m4[6] = quad(-apply(qDt, Et))
    m4[7] = qV
    m4[8] = quad(apply(qD, V))

    loads[0].wait()

    def adjoint_in(xp, carry):
        x = xp * 2
        for c in range(3):
            f = jnp.concatenate([cotv[c, x], cotv[c, x + 1]], axis=1)
            g = apply(m4[1 if c == 2 else 0], f)
            send_z[0, pl.ds(c * 8 + x, 64, stride=24), :] = g[:, :128]
            send_z[0, pl.ds(c * 8 + x + 1, 64, stride=24), :] = g[:, 128:]
        return carry

    lax.fori_loop(0, 4, adjoint_in, 0)

    loads[1].wait()
    lane = lanes((64, 128))

    def pack(x, carry):
        first, last = carry
        for c in range(3):
            f = velp[c, x + 1]
            j = c * 8 + x
            first = jnp.where(lane == j, pltpu.roll(f, j, 1), first)
            last = jnp.where(lane == j, pltpu.roll(f, j + 1, 1), last)
        return first, last

    zero = jnp.zeros((64, 128), f32)
    first, last = lax.fori_loop(0, 8, pack, (zero, zero))
    ycol[0] = first
    ycol[1] = last

    @pl.when(q == part)
    def _():
        pl.semaphore_wait(barrier, 70)

    @pl.when(q != part)
    def _():
        pl.semaphore_wait(barrier, 71)

    def remote(src, dst, ssem, rsem, dev):
        return pltpu.make_async_remote_copy(
            src_ref=src, dst_ref=dst, send_sem=ssem, recv_sem=rsem,
            device_id=dev, device_id_type=MESH,
        )

    halos = [
        remote(velp.at[:, 8], velp.at[:, 0], hx_send.at[0], hx_recv.at[0], east),
        remote(velp.at[:, 1], velp.at[:, 9], hx_send.at[1], hx_recv.at[1], west),
        remote(ycol.at[1], yhalo.at[0], hy_send.at[0], hy_recv.at[0], north),
        remote(ycol.at[0], yhalo.at[1], hy_send.at[1], hy_recv.at[1], south),
    ]
    for copy in halos:
        copy.start()

    def send_levels(e):
        def go(t, carry):
            dz = t % 8
            dx = (t // 8) % 4
            dy = t // 32
            off = (dz % 2) * (4 - (dz + 1) // 2) + (1 - dz % 2) * (4 + dz // 2)
            z = (cz + off) % 8
            x = (cx + dx) % 4
            h = (cy // 2 + dy) % 2
            target = gx_of(x, z, h * 2 + q // 2, q % 2)
            home = (x * 2 + h) * 8 + z
            src = send_z.at[e, pl.ds(pl.multiple_of(home * 24, 8), 24), :]
            dst = recv_x.at[e, gx]
            mine = jnp.logical_and(home == level, q == part)

            @pl.when(mine)
            def _():
                pltpu.make_async_copy(src, dst, big_recv.at[e]).start()

            @pl.when(jnp.logical_not(mine))
            def _():
                remote(src, dst, big_send.at[e], big_recv.at[e], (target, z % 4)).start()

            return carry

        lax.fori_loop(0, 64, go, 0)

    def send_columns(e):
        def go(t, carry):
            h = t % 2
            c = (core + (t // 2) % 2) % 2
            x = (cx + (t // 4) % 4) % 4
            y = (cy + t // 16) % 4
            i = gx_of(x, h * 4, y, c)
            src = back_x.at[e, i]
            dst = back_z.at[e, pl.ds(pl.multiple_of(level * 24, 8), 24), :]
            mine = jnp.logical_and(i == gx, q == part)

            @pl.when(mine)
            def _():
                pltpu.make_async_copy(src, dst, ret_recv.at[e]).start()

            @pl.when(jnp.logical_not(mine))
            def _():
                remote(src, dst, ret_send.at[e], ret_recv.at[e], (i, part)).start()

            return carry

        lax.fori_loop(0, 64, go, 0)

    def all_of(ref, sem):
        pltpu.make_async_copy(ref, ref, sem).wait()

    def swap(e, out, into, ssem, rsem):
        for d in range(1, 4):
            j = (part + d) % 4
            remote(out.at[e, j], into.at[e, part], ssem.at[e], rsem.at[e], member(j)).start()
        pltpu.make_async_copy(out.at[e, part], into.at[e, part], rsem.at[e]).start()

    send_levels(0)

    halos[0].wait_recv()
    halos[1].wait_recv()
    halos[2].wait_recv()
    halos[3].wait_recv()
    loads[2].wait()
    profile = prof[...]

    def section(xp, carry):
        pair = []
        for x in (xp * 2, xp * 2 + 1):
            here = [velp[c, x + 1] for c in range(3)]
            rows = []
            for c in range(3):
                f = here[c]
                e, w = velp[c, x + 2], velp[c, x]
                j = c * 8 + x
                n = jnp.where(lane == 127, pltpu.roll(yhalo[1], 127 - j, 1), pltpu.roll(f, 127, 1))
                s = jnp.where(lane == 0, pltpu.roll(yhalo[0], (128 - j) % 128, 1), pltpu.roll(f, 1, 1))
                laplace = e + w + n + s - 4.0 * f
                lap[c, x] = laplace
                move = here[0] * (0.5 * (e - w)) + here[1] * (0.5 * (n - s))
                rows.append(f + step_weight * (coefv[x] * profile * laplace - move))
            pair.append((here, rows))
        for c in range(3):
            f = jnp.concatenate([pair[0][0][c], pair[1][0][c]], axis=1)
            slope = apply(m4[2], f)
            s = []
            for k in range(2):
                here, rows = pair[k]
                v = rows[c] - step_weight * (here[2] * slope[:, k * 128 : (k + 1) * 128])
                sec[c, xp * 2 + k] = v
                s.append(v)
            g = apply(m4[4 if c == 2 else 3], jnp.concatenate(s, axis=1))
            send_z[1, pl.ds(c * 8 + xp * 2, 64, stride=24), :] = g[:, :128]
            send_z[1, pl.ds(c * 8 + xp * 2 + 1, 64, stride=24), :] = g[:, 128:]
        return carry

    lax.fori_loop(0, 4, section, 0)
    send_levels(1)

    for copy in loads[3:]:
        copy.wait()

    kx_all = lax.broadcasted_iota(jnp.int32, (HALF, 128), 0).astype(f32) * UNIT

    def into_modes(e):
        all_of(recv_x.at[e], big_recv.at[e])
        g = [recv_x[e, :, c * 8 : (c + 1) * 8, :].reshape(N, 128) for c in range(3)]
        high, low = split(jnp.concatenate(g, axis=1))
        modes = dot3(tab[0], tab[1], high, low)
        c0, s0 = modes[:HALF, :128], modes[HALF:, :128]
        uc = modes[:HALF, 256:] + kx_all * s0
        us = modes[HALF:, 256:] - kx_all * c0
        vc, vs = modes[:HALF, 128:256], modes[HALF:, 128:256]
        for j in range(4):
            for r, block in enumerate((uc, us, vc, vs)):
                grp[e, j, r * 64 : (r + 1) * 64, :] = block[j * 64 : (j + 1) * 64]
        swap(e, grp, grp_in, grp_send, grp_recv)

    rate = rates[level]

    def solve(e):
        all_of(grp_in.at[e], grp_recv.at[e])
        high, low = split(jnp.concatenate([grp_in[e, j] for j in range(4)], axis=1))
        spec = dot3(high, low, ttab[0], ttab[1])
        row = lax.broadcasted_iota(jnp.int32, (128, HALF), 0) % 64 + part * 64
        kx = row.astype(f32) * UNIT
        ky = lanes((128, HALF)).astype(f32) * UNIT
        factor = -1.0 / (rate + kx * kx + ky * ky)
        pc = factor * (spec[:128, :HALF] + ky * spec[128:, HALF:])
        ps = factor * (spec[:128, HALF:] - ky * spec[128:, :HALF])
        both = jnp.concatenate(
            [
                jnp.concatenate([pc, ps], axis=1),
                jnp.concatenate([ky * ps, -(ky * pc)], axis=1),
            ],
            axis=0,
        )
        high, low = split(both)
        out = dot3(high, low, tab[0], tab[1])
        for j in range(4):
            bck[e, j] = out[:, j * 128 : (j + 1) * 128]
        swap(e, bck, bck_in, bck_send, bck_recv)

    def from_modes(e):
        all_of(bck_in.at[e], bck_recv.at[e])
        r = [
            jnp.concatenate([bck_in[e, j, k * 64 : (k + 1) * 64, :] for j in range(4)], axis=0)
            for k in range(4)
        ]
        pc, ps, yc, ys = r
        rhs = jnp.concatenate(
            [
                jnp.concatenate([kx_all * ps, yc, pc], axis=1),
                jnp.concatenate([-(kx_all * pc), ys, ps], axis=1),
            ],
            axis=0,
        )
        high, low = split(rhs)
        out = dot3(ttab[0], ttab[1], high, low)
        for c in range(3):
            back_x[e, :, c * 8 : (c + 1) * 8, :] = out[:, c * 128 : (c + 1) * 128].reshape(64, 8, 128)
        send_columns(e)

    into_modes(0)
    into_modes(1)
    solve(0)
    solve(1)
    from_modes(0)
    from_modes(1)

    all_of(back_z.at[0], ret_recv.at[0])

    def levels_of(e, c, x):
        return jnp.concatenate(
            [
                back_z[e, pl.ds(c * 8 + x, 64, stride=24), :],
                back_z[e, pl.ds(c * 8 + x + 1, 64, stride=24), :],
            ],
            axis=1,
        )

    def adjoint_out(xp, carry):
        x = xp * 2
        total = [zero, zero]
        for c in range(3):
            g = apply(m4[6 if c == 2 else 5], levels_of(0, c, x))
            for k in range(2):
                v = cotv[c, x + k] + g[:, k * 128 : (k + 1) * 128]
                cotv[c, x + k] = v
                total[k] = total[k] + v * lap[c, x + k]
        for k in range(2):
            grad[x + k] = step_weight * profile * total[k]
        return carry

    lax.fori_loop(0, 4, adjoint_out, 0)
    outs = [
        pltpu.make_async_copy(cotv, o_adj, out_sem.at[0]),
        pltpu.make_async_copy(grad, o_grad, out_sem.at[1]),
        pltpu.make_async_copy(sec, o_new, out_sem.at[2]),
    ]
    outs[0].start()
    outs[1].start()

    all_of(back_z.at[1], ret_recv.at[1])

    def forward_out(xp, carry):
        x = xp * 2
        for c in range(3):
            g = apply(m4[8 if c == 2 else 7], levels_of(1, c, x))
            for k in range(2):
                sec[c, x + k] = sec[c, x + k] - g[:, k * 128 : (k + 1) * 128]
        return carry

    lax.fori_loop(0, 4, forward_out, 0)
    outs[2].start()

    for copy in halos:
        copy.wait_send()
    for e in range(2):

        @pl.when(q == part)
        def _():
            all_of(recv_x.at[e, pl.ds(0, 63)], big_send.at[e])
            all_of(recv_x.at[e, pl.ds(0, 63)], ret_send.at[e])

        @pl.when(q != part)
        def _():
            all_of(recv_x.at[e], big_send.at[e])
            all_of(recv_x.at[e], ret_send.at[e])

        all_of(grp.at[e, pl.ds(0, 3)], grp_send.at[e])
        all_of(bck.at[e, pl.ds(0, 3)], bck_send.at[e])
    for copy in outs:
        copy.wait()


def body(velocity, cotangent, coefficient, level_profile, vert_deriv, eigen_vectors, eigen_inverse, eigen_rates):
    squares = jnp.stack([vert_deriv, eigen_vectors, eigen_inverse])
    mats = jnp.tile(jnp.concatenate([squares, jnp.swapaxes(squares, 1, 2)], axis=0), (1, 1, 4))
    profile = jnp.broadcast_to(level_profile[:, None], (64, 128))
    tables = [jnp.asarray(t) for t in basis()]
    hbm = pl.BlockSpec(memory_space=pl.ANY)
    vmem = pl.BlockSpec(memory_space=pltpu.VMEM)
    smem = pl.BlockSpec(memory_space=pltpu.SMEM)
    field = (3, 8, 64, 128)
    dma = pltpu.SemaphoreType.DMA
    return pl.pallas_call(
        body_kernel,
        out_shape=(
            jax.ShapeDtypeStruct(field, f32),
            jax.ShapeDtypeStruct(field, f32),
            jax.ShapeDtypeStruct(field[1:], f32),
        ),
        in_specs=[hbm, hbm, hbm, vmem, vmem, smem, hbm, hbm, hbm, hbm],
        out_specs=(hbm, hbm, hbm),
        scratch_shapes=[
            pltpu.VMEM((3, 10, 64, 128), f32),
            pltpu.VMEM(field, f32),
            pltpu.VMEM(field[1:], f32),
            pltpu.VMEM(field, f32),
            pltpu.VMEM(field, f32),
            pltpu.VMEM(field[1:], f32),
            pltpu.VMEM((2, 64, 128), f32),
            pltpu.VMEM((2, 64, 128), f32),
            pltpu.VMEM((2, 1536, 128), f32),
            pltpu.VMEM((2, 64, 24, 128), f32),
            pltpu.VMEM((2, 64, 24, 128), f32),
            pltpu.VMEM((2, 1536, 128), f32),
            pltpu.VMEM((2, 4, 256, 128), f32),
            pltpu.VMEM((2, 4, 256, 128), f32),
            pltpu.VMEM((2, 4, 256, 128), f32),
            pltpu.VMEM((2, 4, 256, 128), f32),
            pltpu.VMEM((2, N, N), bf16),
            pltpu.VMEM((2, N, N), bf16),
            pltpu.VMEM((9, 64, 256), bf16),
            dma((7,)),
            dma((3,)),
            dma((2,)), dma((2,)), dma((2,)), dma((2,)),
            dma((2,)), dma((2,)), dma((2,)), dma((2,)),
            dma((2,)), dma((2,)), dma((2,)), dma((2,)),
        ],
        compiler_params=pltpu.CompilerParams(
            collective_id=0, has_side_effects=True, vmem_limit_bytes=56 << 20
        ),
        name="substep",
    )(velocity, cotangent, coefficient, profile, mats, eigen_rates, *tables)


def solution(mesh):
    field = P(None, "gx", None, "gy")
    cell = P("gx", None, "gy")
    in_specs = (field, field, cell, P(), P(), P(), P(), P())
    return jax.shard_map(body, mesh=mesh, in_specs=in_specs, out_specs=(field, field, cell), check_vma=False)
```

profile of v0, /device:TPU:1, one launch (start us, length us, event | category | flops | bytes accessed | tf_op | source)
XLA Modules:
  0.0 132.4 jit_solution(9661424368750022103)
XLA Ops:
  0.6 0.0 copy-start.3
  0.6 1.3 %broadcast_in_dim.2.prof = f32[64,128]{1,0:T(8,128)} broadcast(f32[64]{0:T(128)} %param.15), dimensions={0} | broadcast | bytes 33024 | tf_op jit(solution)/shard_map/broadcast_in_dim | solution.py:432
  2.0 0.0 copy-done.3
  2.0 0.1 copy.15
  2.1 0.0 copy-start.4
  2.1 0.1 copy.17
  2.1 0.7 copy-done.4
  2.8 0.1 copy.16
  2.9 0.0 copy-start.2
  2.9 0.1 copy.18
  3.0 0.7 copy-done.2
  3.7 0.1 copy.19
  3.8 0.1 copy.20
  3.9 0.1 tile.4
  4.1 1.2 tile.10.mats
  5.3 123.1 %substep.1 = (f32[3,8,64,128]{3,2,1,0:T(8,128)}, f32[3,8,64,128]{3,2,1,0:T(8,128)}, f32[8,64,128]{2,1,0:T(8,128)}) custom-call(f32[3,8,64,128]{3,2,1,0:T(8,128)} %vel.1, f32[3,8,64,128]{3,2,1,0:T(8,128)} %cot.1, f32[8,64,128]{2,1,0:T(8,128)} %coef.1, f32[64,128]{1,0:T(8,128)} %broadcast_in_dim.2.prof, f32[6,64,256]{2,1,0:T(8,128)} %tile.10.mats, f32[64]{0:T(128)} %rates.1, ...), custom_call_target="tpu_custom_call" | custom-call | tf_op jit(solution)/shard_map/substep/pallas_call | solution.py:439
  128.4 0.0 copy-start
  128.4 2.2 %copy.24 = f32[3,8,64,128]{3,2,1,0:T(8,128)} copy(f32[3,8,64,128]{3,2,1,0:T(8,128)} %get-tuple-element.6) | data formatting | bytes 1572864
  130.6 0.0 copy-done
  130.6 0.0 copy-start.1
  130.6 0.9 copy.25
  131.5 0.2 copy-done.1
  131.7 0.7 copy.26
  (2 shorter events, 0.0 us)
Async XLA Ops:
  0.6 1.4 %copy-start.3 = (f32[64,64]{1,0:T(8,128)S(1)}, f32[64,64]{1,0:T(8,128)}, u32[]{:S(2)}) copy-start(f32[64,64]{1,0:T(8,128)} %param.16) | copy-start | bytes 49156
  2.1 0.8 copy-start.4
  2.9 0.8 copy-start.2
  128.4 2.2 %copy-start = (f32[3,8,64,128]{3,2,1,0:T(8,128)S(1)}, f32[3,8,64,128]{3,2,1,0:T(8,128)}, u32[]{:S(2)}) copy-start(f32[3,8,64,128]{3,2,1,0:T(8,128)} %get-tuple-element.7) | copy-start | bytes 2359300
  130.6 1.1 copy-start.1
where the time goes:
time: 133 us; the launch traced here: 132 us
  Pallas kernels  123 us (92%)
  local copies, waits for them, and re-layouts  8.52 us (6%)
    pallas_call x1, Pallas kernels, body(): pl.pallas_call(body_kernel, out_shape=(jax.ShapeDtypeStruct(field, f32),...  123 us
    unnamed x15, local copies, waits for them, and re-layouts  5.48 us

commit v1 on v0

--- a/solution.py
+++ b/solution.py
@@ -13,6 +13,8 @@
 MESH = pl.DeviceIdType.MESH
 step_weight = 0.3 * 8.0 / 15.0
 N = 512
+CUT_F = 32
+CUT_R = 32
 HALF = N // 2
 UNIT = 2.0 * math.pi / N
 f32 = jnp.float32
@@ -79,14 +81,14 @@
     cy = (gx // 2) % 4
     cx = gx // 16
     cz = ((gx // 8) % 2) * 4 + q
-    part = (cy % 2) * 2 + core
+    part = ((cy + cz) % 2) * 2 + core
     level = (cx * 2 + cy // 2) * 8 + cz
 
     def gx_of(x, z, y, c):
         return ((x * 2 + z // 4) * 4 + y) * 2 + c
 
     def member(j):
-        return (gx_of(cx, cz, (cy // 2) * 2 + j // 2, j % 2), q)
+        return (gx_of(cx, cz, (cy // 2) * 2 + (j // 2 + cz) % 2, j % 2), q)
 
     east, west = ((gx + 1) % 64, q), ((gx + 63) % 64, q)
     north, south = (gx, (q + 1) % 4), (gx, (q + 3) % 4)
@@ -188,16 +190,17 @@
     for copy in halos:
         copy.start()
 
-    def send_levels(e):
+    def send_levels(e, start=0, stop=64):
         def go(t, carry):
             dz = t % 8
-            dx = (t // 8) % 4
-            dy = t // 32
+            u = (t // 8 + 2 * part) % 8
+            dx = u % 4
+            dy = u // 4
             off = (dz % 2) * (4 - (dz + 1) // 2) + (1 - dz % 2) * (4 + dz // 2)
             z = (cz + off) % 8
             x = (cx + dx) % 4
             h = (cy // 2 + dy) % 2
-            target = gx_of(x, z, h * 2 + q // 2, q % 2)
+            target = gx_of(x, z, h * 2 + (q // 2 + z) % 2, q % 2)
             home = (x * 2 + h) * 8 + z
             src = send_z.at[e, pl.ds(pl.multiple_of(home * 24, 8), 24), :]
             dst = recv_x.at[e, gx]
@@ -213,14 +216,15 @@
 
             return carry
 
-        lax.fori_loop(0, 64, go, 0)
-
-    def send_columns(e):
+        lax.fori_loop(start, stop, go, 0)
+
+    def send_columns(e, start=0, stop=64):
         def go(t, carry):
-            h = t % 2
-            c = (core + (t // 2) % 2) % 2
-            x = (cx + (t // 4) % 4) % 4
-            y = (cy + t // 16) % 4
+            u = (t + 8 * cz) % 64
+            h = u % 2
+            c = (core + (u // 2) % 2) % 2
+            x = (cx + (u // 4) % 4) % 4
+            y = (cy + u // 16) % 4
             i = gx_of(x, h * 4, y, c)
             src = back_x.at[e, i]
             dst = back_z.at[e, pl.ds(pl.multiple_of(level * 24, 8), 24), :]
@@ -236,7 +240,7 @@
 
             return carry
 
-        lax.fori_loop(0, 64, go, 0)
+        lax.fori_loop(start, stop, go, 0)
 
     def all_of(ref, sem):
         pltpu.make_async_copy(ref, ref, sem).wait()
@@ -287,7 +291,7 @@
         return carry
 
     lax.fori_loop(0, 4, section, 0)
-    send_levels(1)
+    send_levels(1, 0, CUT_F)
 
     for copy in loads[3:]:
         copy.wait()
@@ -351,14 +355,17 @@
         out = dot3(ttab[0], ttab[1], high, low)
         for c in range(3):
             back_x[e, :, c * 8 : (c + 1) * 8, :] = out[:, c * 128 : (c + 1) * 128].reshape(64, 8, 128)
-        send_columns(e)
 
     into_modes(0)
+    send_levels(1, CUT_F, 64)
+    solve(0)
     into_modes(1)
-    solve(0)
+    from_modes(0)
+    send_columns(0, 0, CUT_R)
     solve(1)
-    from_modes(0)
+    send_columns(0, CUT_R, 64)
     from_modes(1)
+    send_columns(1)
 
     all_of(back_z.at[0], ret_recv.at[0])
 

time: 133 us -> 111 us (0.83)
  Pallas kernels: 123 us -> 100 us
    pallas_call x1, Pallas kernels: 123 us -> 100 us  [body(): pl.pallas_call(body_kernel, out_shape=(jax.ShapeDtypeStruct(field, f32),...]
where the time goes in v1:
time: 111 us; the launch traced here: 109 us
  Pallas kernels  100 us (90%)
  local copies, waits for them, and re-layouts  8.52 us (8%)
    pallas_call x1, Pallas kernels, body(): pl.pallas_call(body_kernel, out_shape=(jax.ShapeDtypeStruct(field, f32),...  100 us
    unnamed x15, local copies, waits for them, and re-layouts  5.48 us

profile of v1, /device:TPU:1, one launch (start us, length us, event | category | flops | bytes accessed | tf_op | source)
XLA Modules:
  0.0 109.3 jit_solution(4922320687494435927)
XLA Ops:
  0.6 0.0 copy-start.3
  0.6 1.3 %broadcast_in_dim.2.prof = f32[64,128]{1,0:T(8,128)} broadcast(f32[64]{0:T(128)} %param.15), dimensions={0} | broadcast | bytes 33024 | tf_op jit(solution)/shard_map/broadcast_in_dim | solution.py:439
  2.0 0.0 copy-done.3
  2.0 0.1 copy.15
  2.1 0.0 copy-start.4
  2.1 0.1 copy.17
  2.1 0.7 copy-done.4
  2.8 0.1 copy.16
  2.9 0.0 copy-start.2
  2.9 0.1 copy.18
  3.0 0.7 copy-done.2
  3.7 0.1 copy.19
  3.8 0.1 copy.20
  3.9 0.1 tile.4
  4.1 1.2 %tile.10.mats = f32[6,64,256]{2,1,0:T(8,128)} reshape(f32[6,64,4,64]{3,2,1,0:T(4,128)S(1)} %tile.4) | data formatting | bytes 786432 | tf_op jit(solution)/shard_map/tile | solution.py:438
  5.3 100.1 %substep.1 = (f32[3,8,64,128]{3,2,1,0:T(8,128)}, f32[3,8,64,128]{3,2,1,0:T(8,128)}, f32[8,64,128]{2,1,0:T(8,128)}) custom-call(f32[3,8,64,128]{3,2,1,0:T(8,128)} %vel.1, f32[3,8,64,128]{3,2,1,0:T(8,128)} %cot.1, f32[8,64,128]{2,1,0:T(8,128)} %coef.1, f32[64,128]{1,0:T(8,128)} %broadcast_in_dim.2.prof, f32[6,64,256]{2,1,0:T(8,128)} %tile.10.mats, f32[64]{0:T(128)} %rates.1, ...), custom_call_target="tpu_custom_call" | custom-call | tf_op jit(solution)/shard_map/substep/pallas_call | solution.py:446
  105.3 0.0 copy-start
  105.4 2.2 %copy.24 = f32[3,8,64,128]{3,2,1,0:T(8,128)} copy(f32[3,8,64,128]{3,2,1,0:T(8,128)} %get-tuple-element.6) | data formatting | bytes 1572864
  107.5 0.0 copy-done
  107.5 0.0 copy-start.1
  107.5 0.9 copy.25
  108.4 0.2 copy-done.1
  108.6 0.7 copy.26
  (2 shorter events, 0.0 us)
Async XLA Ops:
  0.6 1.4 %copy-start.3 = (f32[64,64]{1,0:T(8,128)S(1)}, f32[64,64]{1,0:T(8,128)}, u32[]{:S(2)}) copy-start(f32[64,64]{1,0:T(8,128)} %param.16) | copy-start | bytes 49156
  2.1 0.8 copy-start.4
  2.9 0.8 copy-start.2
  105.3 2.2 %copy-start = (f32[3,8,64,128]{3,2,1,0:T(8,128)S(1)}, f32[3,8,64,128]{3,2,1,0:T(8,128)}, u32[]{:S(2)}) copy-start(f32[3,8,64,128]{3,2,1,0:T(8,128)} %get-tuple-element.7) | copy-start | bytes 2359300
  107.5 1.1 copy-start.1

commit v2 on v1

--- a/solution.py
+++ b/solution.py
@@ -55,10 +55,16 @@
     return lax.broadcasted_iota(jnp.int32, shape, len(shape) - 1)
 
 
-def quad(m):
+def quad(m, flip=False):
+    r = lax.broadcasted_iota(jnp.int32, (64, 256), 0)
+    c = lanes((64, 256))
     high, low = split(m)
-    odd = (lanes(m.shape) // 64) % 2 == 1
-    return jnp.where(odd, low.astype(f32), high.astype(f32)).astype(bf16)
+    dims = (((0 if flip else 1,), (0,)), ((), ()))
+    out = 0.0
+    for term, odd in ((high, 0), (low, 1)):
+        pick = jnp.where((c % 64 == r) & ((c // 64) % 2 == odd), 1.0, 0.0).astype(bf16)
+        out = out + lax.dot_general(term, pick, dims, preferred_element_type=f32)
+    return out.astype(bf16)
 
 
 def apply(m4, f):
@@ -67,11 +73,11 @@
 
 
 def body_kernel(
-    vel, cot, coef, prof, mats, rates, t_high, t_low, tt_high, tt_low,
+    vel, cot, coef, deriv, vectors, inverse, prof, rates, t_high, t_low, tt_high, tt_low,
     o_new, o_adj, o_grad,
     velp, cotv, coefv, lap, sec, grad, ycol, yhalo,
     send_z, recv_x, back_x, back_z, grp, grp_in, bck, bck_in,
-    tab, ttab, m4,
+    tab, ttab, mats, m4,
     load_sem, out_sem, hx_send, hx_recv, hy_send, hy_recv,
     big_send, big_recv, grp_send, grp_recv, bck_send, bck_recv, ret_send, ret_recv,
 ):
@@ -93,26 +99,6 @@
     east, west = ((gx + 1) % 64, q), ((gx + 63) % 64, q)
     north, south = (gx, (q + 1) % 4), (gx, (q + 3) % 4)
 
-    barrier = pltpu.get_barrier_semaphore()
-
-    def tell(dev):
-        pl.semaphore_signal(barrier, inc=1, device_id=dev, device_id_type=MESH)
-
-    def tell_source(t, carry):
-        i = (gx + t) % 64
-
-        @pl.when(jnp.logical_or(i != gx, q != part))
-        def _():
-            tell((i, part))
-
-        return carry
-
-    lax.fori_loop(0, 64, tell_source, 0)
-    for d in range(1, 4):
-        tell(member((part + d) % 4))
-    for dev in (east, west, north, south):
-        tell(dev)
-
     loads = [
         pltpu.make_async_copy(cot, cotv, load_sem.at[0]),
         pltpu.make_async_copy(vel, velp.at[:, pl.ds(1, 8)], load_sem.at[1]),
@@ -121,21 +107,40 @@
         pltpu.make_async_copy(t_low, tab.at[1], load_sem.at[4]),
         pltpu.make_async_copy(tt_high, ttab.at[0], load_sem.at[5]),
         pltpu.make_async_copy(tt_low, ttab.at[1], load_sem.at[6]),
+        pltpu.make_async_copy(deriv, mats.at[0], load_sem.at[7]),
+        pltpu.make_async_copy(vectors, mats.at[1], load_sem.at[8]),
+        pltpu.make_async_copy(inverse, mats.at[2], load_sem.at[9]),
     ]
     for copy in loads:
         copy.start()
 
-    D, V, E, Dt, Vt, Et = (mats[i] for i in range(6))
-    qD, qV, qE, qDt, qVt, qEt = (quad(m) for m in (D, V, E, Dt, Vt, Et))
-    m4[0] = quad(-Vt)
-    m4[1] = quad(apply(qVt, Dt))
-    m4[2] = qD
-    m4[3] = qE
-    m4[4] = quad(apply(qE, D))
-    m4[5] = qEt
-    m4[6] = quad(-apply(qDt, Et))
-    m4[7] = qV
-    m4[8] = quad(apply(qD, V))
+    barrier = pltpu.get_barrier_semaphore()
+
+    def tell(dev):
+        pl.semaphore_signal(barrier, inc=1, device_id=dev, device_id_type=MESH)
+
+    def tell_source(t, carry):
+        i = (gx + t) % 64
+
+        @pl.when(jnp.logical_or(i != gx, q != part))
+        def _():
+            tell((i, part))
+
+        return carry
+
+    lax.fori_loop(0, 64, tell_source, 0)
+    for d in range(1, 4):
+        tell(member((part + d) % 4))
+    for dev in (east, west, north, south):
+        tell(dev)
+
+    for copy in loads[7:]:
+        copy.wait()
+    D, V, E = mats[0], mats[1], mats[2]
+    m4[2] = quad(D)
+    DV = apply(m4[2], V)
+    m4[0] = quad(-V, True)
+    m4[1] = quad(DV, True)
 
     loads[0].wait()
 
@@ -194,12 +199,10 @@
         def go(t, carry):
             dz = t % 8
             u = (t // 8 + 2 * part) % 8
-            dx = u % 4
-            dy = u // 4
             off = (dz % 2) * (4 - (dz + 1) // 2) + (1 - dz % 2) * (4 + dz // 2)
             z = (cz + off) % 8
-            x = (cx + dx) % 4
-            h = (cy // 2 + dy) % 2
+            x = (cx + u % 4) % 4
+            h = (cy // 2 + u // 4) % 2
             target = gx_of(x, z, h * 2 + (q // 2 + z) % 2, q % 2)
             home = (x * 2 + h) * 8 + z
             src = send_z.at[e, pl.ds(pl.multiple_of(home * 24, 8), 24), :]
@@ -253,12 +256,22 @@
 
     send_levels(0)
 
+    ED = apply(quad(E), D)
+    m4[3] = quad(E)
+    m4[4] = quad(ED)
+    m4[5] = quad(E, True)
+    m4[6] = quad(-ED, True)
+    m4[7] = quad(V)
+    m4[8] = quad(DV)
+    diagonal = lax.broadcasted_iota(jnp.int32, (64, 64), 0) == lanes((64, 64))
+    column = jnp.sum(jnp.where(diagonal, jnp.broadcast_to(prof[...], (64, 64)), 0.0), axis=1, keepdims=True)
+    profile = jnp.broadcast_to(column, (64, 128))
+
     halos[0].wait_recv()
     halos[1].wait_recv()
     halos[2].wait_recv()
     halos[3].wait_recv()
     loads[2].wait()
-    profile = prof[...]
 
     def section(xp, carry):
         pair = []
@@ -293,7 +306,7 @@
     lax.fori_loop(0, 4, section, 0)
     send_levels(1, 0, CUT_F)
 
-    for copy in loads[3:]:
+    for copy in loads[3:7]:
         copy.wait()
 
     kx_all = lax.broadcasted_iota(jnp.int32, (HALF, 128), 0).astype(f32) * UNIT
@@ -434,9 +447,6 @@
 
 
 def body(velocity, cotangent, coefficient, level_profile, vert_deriv, eigen_vectors, eigen_inverse, eigen_rates):
-    squares = jnp.stack([vert_deriv, eigen_vectors, eigen_inverse])
-    mats = jnp.tile(jnp.concatenate([squares, jnp.swapaxes(squares, 1, 2)], axis=0), (1, 1, 4))
-    profile = jnp.broadcast_to(level_profile[:, None], (64, 128))
     tables = [jnp.asarray(t) for t in basis()]
     hbm = pl.BlockSpec(memory_space=pl.ANY)
     vmem = pl.BlockSpec(memory_space=pltpu.VMEM)
@@ -450,7 +460,7 @@
             jax.ShapeDtypeStruct(field, f32),
             jax.ShapeDtypeStruct(field[1:], f32),
         ),
-        in_specs=[hbm, hbm, hbm, vmem, vmem, smem, hbm, hbm, hbm, hbm],
+        in_specs=[hbm] * 6 + [vmem, smem] + [hbm] * 4,
         out_specs=(hbm, hbm, hbm),
         scratch_shapes=[
             pltpu.VMEM((3, 10, 64, 128), f32),
@@ -471,8 +481,9 @@
             pltpu.VMEM((2, 4, 256, 128), f32),
             pltpu.VMEM((2, N, N), bf16),
             pltpu.VMEM((2, N, N), bf16),
+            pltpu.VMEM((3, 64, 64), f32),
             pltpu.VMEM((9, 64, 256), bf16),
-            dma((7,)),
+            dma((10,)),
             dma((3,)),
             dma((2,)), dma((2,)), dma((2,)), dma((2,)),
             dma((2,)), dma((2,)), dma((2,)), dma((2,)),
@@ -482,7 +493,10 @@
             collective_id=0, has_side_effects=True, vmem_limit_bytes=56 << 20
         ),
         name="substep",
-    )(velocity, cotangent, coefficient, profile, mats, eigen_rates, *tables)
+    )(
+        velocity, cotangent, coefficient, vert_deriv, eigen_vectors, eigen_inverse,
+        level_profile[None, :], eigen_rates, *tables,
+    )
 
 
 def solution(mesh):

time: 111 us -> 106 us (0.955)
  local copies, waits for them, and re-layouts: 8.52 us -> 3.96 us
    another operation x5 -> x0, local copies, waits for them, and re-layouts: 1.58 us -> none  [the longest x2 1.35 us: body(): jnp.tile(jnp.concatenate([squares, jnp.swapaxes(squares, 1, 2)], axis=0),...]
    unnamed x15 -> x7, local copies, waits for them, and re-layouts: 5.48 us -> 3.96 us
    broadcast_in_dim x1 -> x0, local copies, waits for them, and re-layouts: 1.35 us -> none  [body(): profile = jnp.broadcast_to(level_profile[:, None], (64, 128))]
where the time goes in v2:
time: 106 us; the launch traced here: 105 us
  Pallas kernels  100 us (94%)
  local copies, waits for them, and re-layouts  3.96 us (4%)
    pallas_call x1, Pallas kernels, body(): pl.pallas_call(body_kernel, out_shape=(jax.ShapeDtypeStruct(field, f32),...  100 us
    unnamed x7, local copies, waits for them, and re-layouts  3.96 us

profile of v2, /device:TPU:1, one launch (start us, length us, event | category | flops | bytes accessed | tf_op | source)
XLA Modules:
  0.0 104.6 jit_solution(5361693394721087707)
XLA Ops:
  0.6 100.0 %substep.1 = (f32[3,8,64,128]{3,2,1,0:T(8,128)}, f32[3,8,64,128]{3,2,1,0:T(8,128)}, f32[8,64,128]{2,1,0:T(8,128)}) custom-call(f32[3,8,64,128]{3,2,1,0:T(8,128)} %vel.1, f32[3,8,64,128]{3,2,1,0:T(8,128)} %cot.1, f32[8,64,128]{2,1,0:T(8,128)} %coef.1, f32[64,64]{1,0:T(8,128)} %deriv.1, f32[64,64]{1,0:T(8,128)} %vectors.1, f32[64,64]{1,0:T(8,128)} %inverse.1, ...), custom_call_target="tpu_custom_call" | custom-call | tf_op jit(solution)/shard_map/substep/pallas_call | solution.py:456
  100.7 0.0 copy-start
  100.7 2.2 %copy.18 = f32[3,8,64,128]{3,2,1,0:T(8,128)} copy(f32[3,8,64,128]{3,2,1,0:T(8,128)} %get-tuple-element.6) | data formatting | bytes 1572864
  102.8 0.0 copy-done
  102.8 0.0 copy-start.1
  102.8 0.9 copy.19
  103.7 0.2 copy-done.1
  103.9 0.7 copy.20
Async XLA Ops:
  100.7 2.2 %copy-start = (f32[3,8,64,128]{3,2,1,0:T(8,128)S(1)}, f32[3,8,64,128]{3,2,1,0:T(8,128)}, u32[]{:S(2)}) copy-start(f32[3,8,64,128]{3,2,1,0:T(8,128)} %get-tuple-element.7) | copy-start | bytes 2359300
  102.8 1.1 %copy-start.1 = (f32[8,64,128]{2,1,0:T(8,128)S(1)}, f32[8,64,128]{2,1,0:T(8,128)}, u32[]{:S(2)}) copy-start(f32[8,64,128]{2,1,0:T(8,128)} %get-tuple-element.8) | copy-start | bytes 786436

commit v3 on v2

--- a/solution.py
+++ b/solution.py
@@ -446,6 +446,23 @@
         copy.wait()
 
 
+def place_kernel(a, b, c, to_a, to_b, to_c, va, vb, vc, sems):
+    pieces = []
+    for i in range(3):
+        pieces.append((a.at[i], va.at[i], to_a.at[i]))
+        pieces.append((b.at[i], vb.at[i], to_b.at[i]))
+    pieces.append((c, vc, to_c))
+    reads = [pltpu.make_async_copy(p[0], p[1], sems.at[0, i]) for i, p in enumerate(pieces)]
+    writes = [pltpu.make_async_copy(p[1], p[2], sems.at[1, i]) for i, p in enumerate(pieces)]
+    for copy in reads:
+        copy.start()
+    for read, write in zip(reads, writes):
+        read.wait()
+        write.start()
+    for copy in writes:
+        copy.wait()
+
+
 def body(velocity, cotangent, coefficient, level_profile, vert_deriv, eigen_vectors, eigen_inverse, eigen_rates):
     tables = [jnp.asarray(t) for t in basis()]
     hbm = pl.BlockSpec(memory_space=pl.ANY)
@@ -453,13 +470,14 @@
     smem = pl.BlockSpec(memory_space=pltpu.SMEM)
     field = (3, 8, 64, 128)
     dma = pltpu.SemaphoreType.DMA
-    return pl.pallas_call(
+    shapes = (
+        jax.ShapeDtypeStruct(field, f32),
+        jax.ShapeDtypeStruct(field, f32),
+        jax.ShapeDtypeStruct(field[1:], f32),
+    )
+    results = pl.pallas_call(
         body_kernel,
-        out_shape=(
-            jax.ShapeDtypeStruct(field, f32),
-            jax.ShapeDtypeStruct(field, f32),
-            jax.ShapeDtypeStruct(field[1:], f32),
-        ),
+        out_shape=shapes,
         in_specs=[hbm] * 6 + [vmem, smem] + [hbm] * 4,
         out_specs=(hbm, hbm, hbm),
         scratch_shapes=[
@@ -497,6 +515,15 @@
         velocity, cotangent, coefficient, vert_deriv, eigen_vectors, eigen_inverse,
         level_profile[None, :], eigen_rates, *tables,
     )
+    return pl.pallas_call(
+        place_kernel,
+        out_shape=shapes,
+        in_specs=[hbm] * 3,
+        out_specs=(hbm, hbm, hbm),
+        scratch_shapes=[pltpu.VMEM(shape.shape, f32) for shape in shapes] + [dma((2, 7))],
+        compiler_params=pltpu.CompilerParams(vmem_limit_bytes=56 << 20),
+        name="place",
+    )(*results)
 
 
 def solution(mesh):

time: 106 us -> 104 us (0.981)
  local copies, waits for them, and re-layouts: 3.96 us -> 0 us
  Pallas kernels: 100 us -> 102 us
    unnamed x7 -> x0, local copies, waits for them, and re-layouts: 3.96 us -> none
    pallas_call x1 -> x2, Pallas kernels: 100 us -> 102 us  [the longest x1 100 us: body(): pl.pallas_call(body_kernel, out_shape=shapes, in_specs=[hbm] * 6 + [vmem,...]
where the time goes in v3:
time: 104 us; the launch traced here: 103 us
  Pallas kernels  102 us (98%)
    pallas_call x1, Pallas kernels, body(): pl.pallas_call(body_kernel, out_shape=shapes, in_specs=[hbm] * 6 + [vmem,...  100 us
    pallas_call x1, Pallas kernels, body(): pl.pallas_call(place_kernel, out_shape=shapes, in_specs=[hbm] * 3, out_sp...  2.29 us

profile of v3, /device:TPU:1, one launch (start us, length us, event | category | flops | bytes accessed | tf_op | source)
XLA Modules:
  0.0 102.9 jit_solution(9560950196570012546)
XLA Ops:
  0.6 100.0 %substep.1 = (f32[3,8,64,128]{3,2,1,0:T(8,128)}, f32[3,8,64,128]{3,2,1,0:T(8,128)}, f32[8,64,128]{2,1,0:T(8,128)}) custom-call(f32[3,8,64,128]{3,2,1,0:T(8,128)} %vel.1, f32[3,8,64,128]{3,2,1,0:T(8,128)} %cot.1, f32[8,64,128]{2,1,0:T(8,128)} %coef.1, f32[64,64]{1,0:T(8,128)} %deriv.1, f32[64,64]{1,0:T(8,128)} %vectors.1, f32[64,64]{1,0:T(8,128)} %inverse.1, ...), custom_call_target="tpu_custom_call" | custom-call | tf_op jit(solution)/shard_map/substep/pallas_call | solution.py:478
  100.6 2.3 %place.1 = (f32[3,8,64,128]{3,2,1,0:T(8,128)}, f32[3,8,64,128]{3,2,1,0:T(8,128)}, f32[8,64,128]{2,1,0:T(8,128)}) custom-call(f32[3,8,64,128]{3,2,1,0:T(8,128)} %get-tuple-element.6.a, f32[3,8,64,128]{3,2,1,0:T(8,128)} %get-tuple-element.7.b, f32[8,64,128]{2,1,0:T(8,128)} %get-tuple-element.8.c), custom_call_target="tpu_custom_call" | custom-call | tf_op jit(solution)/shard_map/place/pallas_call | solution.py:518

commit v4 on v3

--- a/solution.py
+++ b/solution.py
@@ -249,7 +249,7 @@
         pltpu.make_async_copy(ref, ref, sem).wait()
 
     def swap(e, out, into, ssem, rsem):
-        for d in range(1, 4):
+        for d in (2, 1, 3):
             j = (part + d) % 4
             remote(out.at[e, j], into.at[e, part], ssem.at[e], rsem.at[e], member(j)).start()
         pltpu.make_async_copy(out.at[e, part], into.at[e, part], rsem.at[e]).start()
@@ -421,10 +421,10 @@
             g = apply(m4[8 if c == 2 else 7], levels_of(1, c, x))
             for k in range(2):
                 sec[c, x + k] = sec[c, x + k] - g[:, k * 128 : (k + 1) * 128]
+        pltpu.make_async_copy(sec.at[:, pl.ds(x, 2)], o_new.at[:, pl.ds(x, 2)], out_sem.at[2]).start()
         return carry
 
     lax.fori_loop(0, 4, forward_out, 0)
-    outs[2].start()
 
     for copy in halos:
         copy.wait_send()

time: 104 us -> 107 us (1.029); the launches traced: 103 us -> 107 us
  Pallas kernels: 102 us -> 106 us
    pallas_call x1, Pallas kernels: 100 us -> 104 us  [body(): pl.pallas_call(body_kernel, out_shape=shapes, in_specs=[hbm] * 6 + [vmem,...]
where the time goes in v4:
time: 107 us
  Pallas kernels  106 us (99%)
    pallas_call x1, Pallas kernels, body(): pl.pallas_call(body_kernel, out_shape=shapes, in_specs=[hbm] * 6 + [vmem,...  104 us
    pallas_call x1, Pallas kernels, body(): pl.pallas_call(place_kernel, out_shape=shapes, in_specs=[hbm] * 3, out_sp...  2.29 us

profile of v4, /device:TPU:1, one launch (start us, length us, event | category | flops | bytes accessed | tf_op | source)
XLA Modules:
  0.0 107.1 jit_solution(12998785137024389029)
XLA Ops:
  0.6 104.2 %substep.1 = (f32[3,8,64,128]{3,2,1,0:T(8,128)}, f32[3,8,64,128]{3,2,1,0:T(8,128)}, f32[8,64,128]{2,1,0:T(8,128)}) custom-call(f32[3,8,64,128]{3,2,1,0:T(8,128)} %vel.1, f32[3,8,64,128]{3,2,1,0:T(8,128)} %cot.1, f32[8,64,128]{2,1,0:T(8,128)} %coef.1, f32[64,64]{1,0:T(8,128)} %deriv.1, f32[64,64]{1,0:T(8,128)} %vectors.1, f32[64,64]{1,0:T(8,128)} %inverse.1, ...), custom_call_target="tpu_custom_call" | custom-call | tf_op jit(solution)/shard_map/substep/pallas_call | solution.py:478
  104.8 2.3 %place.1 = (f32[3,8,64,128]{3,2,1,0:T(8,128)}, f32[3,8,64,128]{3,2,1,0:T(8,128)}, f32[8,64,128]{2,1,0:T(8,128)}) custom-call(f32[3,8,64,128]{3,2,1,0:T(8,128)} %get-tuple-element.6.a, f32[3,8,64,128]{3,2,1,0:T(8,128)} %get-tuple-element.7.b, f32[8,64,128]{2,1,0:T(8,128)} %get-tuple-element.8.c), custom_call_target="tpu_custom_call" | custom-call | tf_op jit(solution)/shard_map/place/pallas_call | solution.py:518
